TPU v7x, 32 devices: a whole 2x2x4 slice. The times are simulated.
32 devices in a mesh: wide: 8 (over z, x), narrow: 4 (over y, core).
Axes of the slice: x: 2, y: 2, z: 4, core: 2. Of those that a mesh axis runs over, the one named last changes fastest.
Arguments:
- patches: bfloat16 [4096, 256], P(('wide', 'narrow')), may hold values from -6 to 6
- token_kind: int32 [4096], P(('wide', 'narrow')), may hold values 0 or 1
- mask_slots: int32 [16, 64], P('wide'), may hold values from 0 to 255
- projector: bfloat16 [2, 256, 768], replicated, may hold values from -0.375 to 0.375
- offsets: bfloat16 [2, 768], replicated, may hold values from -3 to 3
- placeholder: bfloat16 [768], replicated, may hold values from -4 to 4
- positions: bfloat16 [256, 768], replicated, may hold values from -3 to 3
- scales: bfloat16 [2, 2, 768], replicated, may hold values from 0.5 to 1.5
- shifts: bfloat16 [2, 2, 768], replicated, may hold values from -3 to 3
- attention: bfloat16 [2, 3, 768, 768], P(None, None, None, 'narrow'), may hold values from -0.21875 to 0.21875
- attn_bias: bfloat16 [2, 2, 768], P(None, None, 'narrow'), may hold values from -3 to 3
- combiner: bfloat16 [2, 768, 768], P(None, 'narrow'), may hold values from -1.75 to 1.75
- comb_bias: bfloat16 [2, 768], replicated, may hold values from -3 to 3
- expander: bfloat16 [2, 768, 3072], P(None, None, 'narrow'), may hold values from -0.21875 to 0.21875
- expand_bias: bfloat16 [2, 3072], P(None, 'narrow'), may hold values from -3 to 3
- reducer: bfloat16 [2, 3072, 768], P(None, 'narrow'), may hold values from -0.15625 to 0.15625
- reduce_bias: bfloat16 [2, 768], replicated, may hold values from -3 to 3
- cotangent: bfloat16 [4096, 768], P(('wide', 'narrow')), may hold values from -6 to 6
Outputs:
- encoded: float32 [4096, 768], P(('wide', 'narrow'))
- grad_patches: float32 [4096, 256], P(('wide', 'narrow'))
- grad_projector: float32 [2, 256, 768], replicated
- grad_offsets: float32 [2, 768], replicated
- grad_placeholder: float32 [768], replicated
- grad_positions: float32 [256, 768], replicated
- grad_scales: float32 [2, 2, 768], replicated
- grad_shifts: float32 [2, 2, 768], replicated
- grad_attention: float32 [2, 3, 768, 768], P(None, None, None, 'narrow')
- grad_attnbias: float32 [2, 2, 768], P(None, None, 'narrow')
- grad_combiner: float32 [2, 768, 768], P(None, 'narrow')
- grad_combbias: float32 [2, 768], replicated
- grad_expander: float32 [2, 768, 3072], P(None, None, 'narrow')
- grad_expbias: float32 [2, 3072], P(None, 'narrow')
- grad_reducer: float32 [2, 3072, 768], P(None, 'narrow')
- grad_redbias: float32 [2, 768], replicated
Inputs may be any that keep to these rules, and one draw needn't show every extreme that they name: `mask_slots`: positions within the clip; a position may appear more than once.
All inputs are finite; a program needn't handle non-finite values. No bound on the sum of `token_kind` on one device may be relied on, other than what follows from the above.
Results may differ from a plain program's by a relative error of at most 0.025.
Values may be sent and summed in bfloat16 or wider, within the bound.
A program may use at most 128 MiB of HBM per device.

v0:
```python
from functools import partial
import math
import jax
import jax.numpy as jnp
from jax import lax
from jax.sharding import PartitionSpec as P

HD = 64
norm_eps = 1e-06


def normalize(values, gain, shift):
    center = values - jnp.mean(values, axis=-1, keepdims=True)
    variance = jnp.mean(center * center, axis=-1, keepdims=True)
    return center * lax.rsqrt(variance + norm_eps) * gain + shift


def norm_params(values, grad):
    center = values - jnp.mean(values, axis=-1, keepdims=True)
    variance = jnp.mean(center * center, axis=-1, keepdims=True)
    hat = center * lax.rsqrt(variance + norm_eps)
    return (jnp.sum(grad * hat, axis=0), jnp.sum(grad, axis=0))


def share_rows(values):
    return lax.all_gather(values, "narrow", axis=0, tiled=True)


def share_grads(values):
    return lax.all_gather(values, "narrow", axis=0, tiled=True)


def sum_forward(source, weight, local_rows):

    def term(start, count):
        return jnp.dot(source, weight, preferred_element_type=jnp.float32)

    return lax.psum_scatter(
        term(jnp.int32(0), local_rows * lax.axis_size("narrow")).astype(jnp.bfloat16),
        "narrow",
        scatter_dimension=0,
        tiled=True,
    ).astype(jnp.float32)


def sum_backward(source, weight, local_rows):

    def term(start, count):
        return jnp.einsum("rk,dk->rd", source, weight, preferred_element_type=jnp.float32)

    return lax.psum_scatter(
        term(jnp.int32(0), local_rows * lax.axis_size("narrow")).astype(jnp.bfloat16),
        "narrow",
        scatter_dimension=0,
        tiled=True,
    ).astype(jnp.float32)


def attend_block(inputs):
    query, key, value = inputs
    scores = jnp.einsum("bqhd,bkhd->bhqk", query, key, preferred_element_type=jnp.float32)
    top = jnp.max(scores, axis=-1, keepdims=True)
    raised = jnp.exp(scores - top)
    total = jnp.sum(raised, axis=-1, keepdims=True)
    weights = raised / total
    mixed = jnp.einsum(
        "bhqk,bkhd->bqhd", weights.astype(jnp.bfloat16), value, preferred_element_type=jnp.float32
    )
    return (mixed.astype(jnp.bfloat16), top + jnp.log(total))


def attend_back(inputs):
    query, key, value, log_total, grad_mixed = inputs
    scores = jnp.einsum("bqhd,bkhd->bhqk", query, key, preferred_element_type=jnp.float32)
    weights = jnp.exp(scores - log_total)
    grad_weights = jnp.einsum(
        "bqhd,bkhd->bhqk", grad_mixed, value, preferred_element_type=jnp.float32
    )
    grad_value = jnp.einsum(
        "bhqk,bqhd->bkhd",
        weights.astype(jnp.bfloat16),
        grad_mixed,
        preferred_element_type=jnp.float32,
    ).astype(jnp.bfloat16)
    center = jnp.sum(weights * grad_weights, axis=-1, keepdims=True)
    grad_scores = (weights * (grad_weights - center)).astype(jnp.bfloat16)
    grad_query = jnp.einsum(
        "bhqk,bkhd->bqhd", grad_scores, key, preferred_element_type=jnp.float32
    ).astype(jnp.bfloat16)
    grad_key = jnp.einsum(
        "bhqk,bqhd->bkhd", grad_scores, query, preferred_element_type=jnp.float32
    ).astype(jnp.bfloat16)
    return (grad_query, grad_key, grad_value)


def per_device(
    patches,
    token_kind,
    mask_slots,
    projector,
    offsets,
    placeholder,
    positions,
    scales,
    shifts,
    attention,
    attn_bias,
    combiner,
    comb_bias,
    expander,
    expand_bias,
    reducer,
    reduce_bias,
    cotangent,
):
    local_rows, patch_len = patches.shape
    width = projector.shape[2]
    clip_count = mask_slots.shape[0]
    seq_len = positions.shape[0]
    group_rows = clip_count * seq_len
    start_row = lax.axis_index("narrow") * local_rows
    head_cols = attention.shape[3]
    local_heads = head_cols // HD
    layer_count = scales.shape[0]
    scale = HD ** (-0.5)
    block_clips = math.gcd(clip_count, max(1, 512 // seq_len))
    block_count = clip_count // block_clips
    head_shape = (block_count, block_clips, seq_len, local_heads, HD)
    place = jnp.arange(seq_len, dtype=jnp.int32)
    masked_group = jnp.any(mask_slots[:, :, None] == place[None, None, :], axis=1).reshape(
        group_rows, 1
    )
    masked = lax.dynamic_slice_in_dim(masked_group, start_row, local_rows, 0)
    is_patch = (token_kind == 1).reshape(local_rows, 1)
    blank = jnp.zeros_like(patches)
    widened = jnp.concatenate(
        [jnp.where(is_patch, blank, patches), jnp.where(is_patch, patches, blank)], axis=1
    )
    flat_projector = projector.reshape(2 * patch_len, width)
    lifted = jnp.dot(widened, flat_projector, preferred_element_type=jnp.float32)
    shifted = lifted + jnp.where(
        is_patch, offsets[1].astype(jnp.float32), offsets[0].astype(jnp.float32)
    )
    table = jnp.broadcast_to(positions.astype(jnp.float32)[None], (clip_count, seq_len, width))
    position_rows = lax.dynamic_slice_in_dim(
        table.reshape(group_rows, width), start_row, local_rows, 0
    )
    stream = jnp.where(masked, placeholder.astype(jnp.float32), shifted) + position_rows
    grad_top = cotangent.astype(jnp.float32)
    saved = []
    for layer in range(layer_count):
        first = normalize(
            stream, scales[layer, 0].astype(jnp.float32), shifts[layer, 0].astype(jnp.float32)
        ).astype(jnp.bfloat16)
        first_all = share_rows(first)
        joined = attention[layer].transpose(1, 0, 2).reshape(width, 3 * head_cols)
        triple = jnp.dot(first_all, joined, preferred_element_type=jnp.float32)
        query = ((triple[:, :head_cols] + attn_bias[layer, 0].astype(jnp.float32)) * scale).astype(
            jnp.bfloat16
        )
        key = triple[:, head_cols : 2 * head_cols].astype(jnp.bfloat16)
        value = (triple[:, 2 * head_cols :] + attn_bias[layer, 1].astype(jnp.float32)).astype(
            jnp.bfloat16
        )
        mixed, log_total = lax.map(
            attend_block,
            (query.reshape(head_shape), key.reshape(head_shape), value.reshape(head_shape)),
        )
        mixed = mixed.reshape(group_rows, head_cols)
        middle = (
            stream
            + sum_forward(mixed, combiner[layer], local_rows)
            + comb_bias[layer].astype(jnp.float32)
        )
        second = normalize(
            middle, scales[layer, 1].astype(jnp.float32), shifts[layer, 1].astype(jnp.float32)
        ).astype(jnp.bfloat16)
        second_all = share_rows(second)
        pre_act = jnp.dot(
            second_all, expander[layer], preferred_element_type=jnp.float32
        ) + expand_bias[layer].astype(jnp.float32)
        hidden = jax.nn.gelu(pre_act, approximate=False).astype(jnp.bfloat16)
        saved.append(
            (
                stream,
                first_all,
                query,
                key,
                value,
                log_total,
                mixed,
                middle,
                second_all,
                pre_act,
                hidden,
            )
        )
        stream = (
            middle
            + sum_forward(hidden, reducer[layer], local_rows)
            + reduce_bias[layer].astype(jnp.float32)
        )
    grad_stream = grad_top
    owned = [None] * layer_count
    gain_grads = [None] * layer_count
    shift_grads = [None] * layer_count
    comb_grads = [None] * layer_count
    red_grads = [None] * layer_count
    for layer in reversed(range(layer_count)):
        (
            stream_in,
            first_all,
            query,
            key,
            value,
            log_total,
            mixed,
            middle,
            second_all,
            pre_act,
            hidden,
        ) = saved[layer]
        red_grads[layer] = jnp.sum(grad_stream, axis=0)
        out_round = share_grads(grad_stream.astype(jnp.bfloat16))
        grad_reducer = jnp.einsum(
            "rf,rd->fd", hidden, out_round, preferred_element_type=jnp.float32
        )
        grad_hidden = jnp.einsum(
            "rd,fd->rf", out_round, reducer[layer], preferred_element_type=jnp.float32
        )
        _, gelu_back = jax.vjp(partial(jax.nn.gelu, approximate=False), pre_act)
        grad_pre = gelu_back(grad_hidden)[0]
        grad_expbias = jnp.sum(grad_pre, axis=0)
        pre_round = grad_pre.astype(jnp.bfloat16)
        grad_expander = jnp.einsum(
            "rd,rf->df", second_all, pre_round, preferred_element_type=jnp.float32
        )
        grad_second = sum_backward(pre_round, expander[layer], local_rows)
        _, norm_back = jax.vjp(
            normalize,
            middle,
            scales[layer, 1].astype(jnp.float32),
            shifts[layer, 1].astype(jnp.float32),
        )
        grad_mid_in = norm_back(grad_second)[0]
        grad_gain_two, grad_shift_two = norm_params(middle, grad_second)
        grad_middle = grad_stream + grad_mid_in
        comb_grads[layer] = jnp.sum(grad_middle, axis=0)
        mid_round = share_grads(grad_middle.astype(jnp.bfloat16))
        grad_combiner = jnp.einsum(
            "re,rd->ed", mixed, mid_round, preferred_element_type=jnp.float32
        )
        grad_mixed = jnp.einsum(
            "rd,ed->re", mid_round, combiner[layer], preferred_element_type=jnp.float32
        ).astype(jnp.bfloat16)
        grad_query, grad_key, grad_value = lax.map(
            attend_back,
            (
                query.reshape(head_shape),
                key.reshape(head_shape),
                value.reshape(head_shape),
                log_total,
                grad_mixed.reshape(head_shape),
            ),
        )
        grad_query = grad_query.reshape(group_rows, head_cols) * scale
        grad_value = grad_value.reshape(group_rows, head_cols)
        grad_triple = jnp.concatenate(
            [grad_query, grad_key.reshape(group_rows, head_cols), grad_value], axis=1
        )
        grad_joined = jnp.einsum(
            "rd,rk->dk", first_all, grad_triple, preferred_element_type=jnp.float32
        )
        grad_attention = grad_joined.reshape(width, 3, head_cols).transpose(1, 0, 2)
        grad_attnbias = jnp.stack(
            [
                jnp.sum(grad_query.astype(jnp.float32), axis=0),
                jnp.sum(grad_value.astype(jnp.float32), axis=0),
            ]
        )
        joined = attention[layer].transpose(1, 0, 2).reshape(width, 3 * head_cols)
        grad_first = sum_backward(grad_triple, joined, local_rows)
        _, norm_back = jax.vjp(
            normalize,
            stream_in,
            scales[layer, 0].astype(jnp.float32),
            shifts[layer, 0].astype(jnp.float32),
        )
        grad_in = norm_back(grad_first)[0]
        grad_gain_one, grad_shift_one = norm_params(stream_in, grad_first)
        grad_stream = grad_middle + grad_in
        gain_grads[layer] = jnp.stack([grad_gain_one, grad_gain_two])
        shift_grads[layer] = jnp.stack([grad_shift_one, grad_shift_two])
        own_grads = (
            grad_attention,
            grad_attnbias,
            grad_combiner,
            grad_expander,
            grad_expbias,
            grad_reducer,
        )
        own_grads = lax.psum(
            (
                grad_attention,
                grad_attnbias,
                grad_combiner,
                grad_expander,
                grad_expbias,
                grad_reducer,
            ),
            "wide",
        )
        owned[layer] = own_grads
    sum_attention, sum_attnbias, sum_combiner, sum_expander, sum_expbias, sum_reducer = [
        jnp.stack([owned[layer][index] for layer in range(layer_count)]) for index in range(6)
    ]
    spread_rows = lax.dynamic_update_slice_in_dim(
        jnp.zeros((group_rows, width), jnp.float32), grad_stream, start_row, 0
    )
    grad_positions = jnp.sum(spread_rows.reshape(clip_count, seq_len, width), axis=0)
    grad_placeholder = jnp.sum(jnp.where(masked, grad_stream, 0.0), axis=0)
    grad_lifted = jnp.where(masked, 0.0, grad_stream)
    grad_offsets = jnp.stack(
        [
            jnp.sum(jnp.where(is_patch, 0.0, grad_lifted), axis=0),
            jnp.sum(jnp.where(is_patch, grad_lifted, 0.0), axis=0),
        ]
    )
    lifted_round = grad_lifted.astype(jnp.bfloat16)
    grad_projector = jnp.einsum(
        "rp,rd->pd", widened, lifted_round, preferred_element_type=jnp.float32
    ).reshape(2, patch_len, width)
    both_halves = jnp.einsum(
        "rd,pd->rp", lifted_round, flat_projector, preferred_element_type=jnp.float32
    )
    grad_patches = jnp.where(is_patch, both_halves[:, patch_len:], both_halves[:, :patch_len])
    grad_scales = jnp.stack(gain_grads)
    grad_shifts = jnp.stack(shift_grads)
    grad_combbias = jnp.stack(comb_grads)
    grad_redbias = jnp.stack(red_grads)
    (
        grad_scales,
        grad_shifts,
        grad_combbias,
        grad_redbias,
        grad_projector,
        grad_offsets,
        grad_placeholder,
        grad_positions,
    ) = lax.psum(
        (
            grad_scales,
            grad_shifts,
            grad_combbias,
            grad_redbias,
            grad_projector,
            grad_offsets,
            grad_placeholder,
            grad_positions,
        ),
        ("wide", "narrow"),
    )
    return (
        stream,
        grad_patches,
        grad_projector,
        grad_offsets,
        grad_placeholder,
        grad_positions,
        grad_scales,
        grad_shifts,
        sum_attention,
        sum_attnbias,
        sum_combiner,
        grad_combbias,
        sum_expander,
        sum_expbias,
        sum_reducer,
        grad_redbias,
    )


def solution(mesh):
    return jax.shard_map(
        per_device,
        mesh=mesh,
        in_specs=(
            P(("wide", "narrow"), None),
            P(("wide", "narrow")),
            P("wide", None),
            P(),
            P(),
            P(),
            P(),
            P(),
            P(),
            P(None, None, None, "narrow"),
            P(None, None, "narrow"),
            P(None, "narrow", None),
            P(),
            P(None, None, "narrow"),
            P(None, "narrow"),
            P(None, "narrow", None),
            P(),
            P(("wide", "narrow"), None),
        ),
        out_specs=(
            P(("wide", "narrow"), None),
            P(("wide", "narrow"), None),
            P(),
            P(),
            P(),
            P(),
            P(),
            P(),
            P(None, None, None, "narrow"),
            P(None, None, "narrow"),
            P(None, "narrow", None),
            P(),
            P(None, None, "narrow"),
            P(None, "narrow"),
            P(None, "narrow", None),
            P(),
        ),
        check_vma=False,
    )
```

profile of v0, /device:TPU:0, one launch (start us, length us, event | category | flops | bytes accessed | tf_op | source)
XLA Modules:
  0.0 964.3 jit_solution(6585855473328736234)
XLA Ops:
  15.2 10.1 %all_gather.24 = bf16[512,768]{1,0:T(8,128)(2,1)S(1)} all-gather(bf16[128,768]{1,0:T(8,128)(2,1)S(1)} %add_convert_fusion.3), channel_id=1, replica_groups=mesh['wide'=8,'narrow'=4] {'narrow'}, dimensions={0}, use_global_device_ids=true | all-gather | bytes 983040 | tf_op jit(solution)/shard_map/all_gather | solution.py:26
  32.6 23.0 %reduce-scatter.9.cloned.1.call-done = bf16[128,768]{1,0:T(8,128)(2,1)} async-done(((bf16[512,768]{1,0:T(8,128)(2,1)}), bf16[128,768]{1,0:T(8,128)(2,1)}) %reduce-scatter.9.cloned.1.call-update) | async-done | bytes 196624 | tf_op jit(solution)/shard_map/reduce_scatter | solution.py:38
  57.1 8.2 all_gather.25
  65.4 5.4 multiply_convert_fusion.3
  74.1 23.1 %reduce-scatter.11.cloned.1.call-done = bf16[128,768]{1,0:T(8,128)(2,1)} async-done(((bf16[512,768]{1,0:T(8,128)(2,1)}), bf16[128,768]{1,0:T(8,128)(2,1)}) %reduce-scatter.11.cloned.1.call-update) | async-done | bytes 196624 | tf_op jit(solution)/shard_map/reduce_scatter | solution.py:38
  98.8 8.2 all_gather.26
  122.2 10.1 %all_gather.28 = bf16[512,768]{1,0:T(8,128)(2,1)} all-gather(bf16[128,768]{1,0:T(8,128)(2,1)} %param.35), channel_id=1, replica_groups=mesh['wide'=8,'narrow'=4] {'narrow'}, dimensions={0}, use_global_device_ids=true | all-gather | bytes 983040 | tf_op jit(solution)/shard_map/all_gather | solution.py:30
  132.3 13.6 %reduce-scatter.13.cloned.1.call-done = bf16[128,768]{1,0:T(8,128)(2,1)} async-done(((bf16[512,768]{1,0:T(8,128)(2,1)}), bf16[128,768]{1,0:T(8,128)(2,1)}) %reduce-scatter.13.cloned.1.call-update) | async-done | bytes 196624 | tf_op jit(solution)/shard_map/reduce_scatter | solution.py:38
  148.0 8.7 all_gather.27
  156.8 10.9 %multiply_convert_fusion.2 = (bf16[512,768]{1,0:T(8,128)(2,1)}, f32[512,768]{1,0:T(8,128)S(1)}, f32[512,768]{1,0:T(8,128)S(1)}) fusion(f32[768]{0:T(1024)S(1)} %copy-done.119, bf16[512,768]{1,0:T(8,128)(2,1)S(1)} %all_gather.27, bf16[2,768,768]{2,1,0:T(8,128)(2,1)S(1)} %copy-done.133), kind=kOutput, calls=%fused_computation.19 | convolution fusion | flops 629932032 | bytes 5902336 | tf_op jit(solution)/shard_map/dot_general | solution.py:179
  172.1 3.2 convolution_convert_fusion.2
  176.2 19.7 %reduce-scatter.17.cloned.1.call-done = bf16[128,768]{1,0:T(8,128)(2,1)} async-done(((bf16[512,768]{1,0:T(8,128)(2,1)}), bf16[128,768]{1,0:T(8,128)(2,1)}) %reduce-scatter.17.cloned.1.call-update) | async-done | bytes 196624 | tf_op jit(solution)/shard_map/reduce_scatter | solution.py:51
  198.9 22.7 %reduce-scatter.15.cloned.1.call-done = bf16[128,768]{1,0:T(8,128)(2,1)} async-done(((bf16[512,768]{1,0:T(8,128)(2,1)}), bf16[128,768]{1,0:T(8,128)(2,1)}) %reduce-scatter.15.cloned.1.call-update) | async-done | bytes 196624 | tf_op jit(solution)/shard_map/reduce_scatter | solution.py:38
  224.6 8.2 all_gather.29
  236.5 2.7 convert_reduce_fusion.5
  245.3 23.8 %reduce-scatter.19.cloned.1.call-done = bf16[128,768]{1,0:T(8,128)(2,1)} async-done(((bf16[512,768]{1,0:T(8,128)(2,1)}), bf16[128,768]{1,0:T(8,128)(2,1)}) %reduce-scatter.19.cloned.1.call-update) | async-done | bytes 196624 | tf_op jit(solution)/shard_map/reduce_scatter | solution.py:51
  276.2 8.4 all_gather.30
  284.6 3.5 fusion.133
  290.9 3.6 convolution_bitcast_fusion.2
  294.5 20.1 %reduce-scatter.21.cloned.1.call-done = bf16[128,768]{1,0:T(8,128)(2,1)} async-done(((bf16[512,768]{1,0:T(8,128)(2,1)}), bf16[128,768]{1,0:T(8,128)(2,1)}) %reduce-scatter.21.cloned.1.call-update) | async-done | bytes 196624 | tf_op jit(solution)/shard_map/reduce_scatter | solution.py:51
  320.1 8.2 all_gather.31
  337.8 3.4 convolution_bitcast_fusion
  346.9 2.2 convolution_bitcast_fusion.1
  356.1 38.3 %all-reduce.2 = (f32[1,2,192]{2,1,0:T(2,128)S(1)}, f32[1,2,192]{2,1,0:T(2,128)S(1)}, f32[1,768]{1,0:T(1,128)S(1)}, f32[1,768]{1,0:T(1,128)S(1)}) all-reduce(f32[1,2,192]{2,1,0:T(2,128)S(1)} %maximum_bitcast_fusion.5, f32[1,2,192]{2,1,0:T(2,128)S(1)} %maximum_bitcast_fusion.4, ...), channel_id=1, replica_groups=mesh['wide'=8,'narrow'=4] {'wide'}, use_global_device_ids=true, to_apply=%region_56.57 | all-reduce | flops 2304 | bytes 18432 | tf_op jit(solution)/shard_map/psum | solution.py:302
  405.3 43.3 %all-reduce = (f32[2,768]{1,0:T(2,128)}, f32[768]{0:T(1024)}, f32[2,2,768]{2,1,0:T(2,128)}, f32[2,2,768]{2,1,0:T(2,128)}, f32[2,768]{1,0:T(2,128)}, /*index=5*/f32[2,768]{1,0:T(2,128)}) all-reduce(f32[2,768]{1,0:T(2,128)S(1)} %pad_maximum_fusion.9, ...), channel_id=1, replica_groups=mesh['wide'=8,'narrow'=4] {'wide','narrow'}, use_global_device_ids=true, to_apply=%region_34.35 | all-reduce | flops 11520 | bytes 92160 | tf_op jit(solution)/shard_map/psum | solution.py:350
  449.8 363.5 %all-reduce.9.cloned.1.call-done = (f32[1,3,768,192]{2,3,1,0:T(8,128)}, f32[1,3,768,192]{2,3,1,0:T(8,128)}, f32[1,192,768]{2,1,0:T(8,128)}, f32[1,192,768]{2,1,0...) async-done(((f32[1,3,768,192]{2,3,1,0:T(8,128)}, f32[1,3,768,192]{2,3,1,0:T(8,128)}, ...) | async-done | bytes 14155792 | tf_op jit(solution)/shard_map/psum | solution.py:302
  813.3 2.5 pad_maximum_fusion.3
  815.8 3.7 pad_maximum_fusion.2
  819.5 2.7 pad_maximum_fusion
  823.6 2.5 pad_maximum_fusion.1
  826.1 127.5 %all-reduce.7.cloned.1.call-done = (f32[2,256,768]{2,1,0:T(8,128)}, f32[256,768]{1,0:T(8,128)}) async-done(((f32[2,256,768]{2,1,0:T(8,128)}, f32[256,768]{1,0:T(8,128)}), (f32[2,256,768]{2,1,0:T(8,128)}, f32[256,768]{1,0:T(8,128)})) %all-reduce.7.cloned.1.call-update) | async-done | bytes 2359312 | tf_op jit(solution)/shard_map/psum | solution.py:350
  953.6 2.7 copy.210
  (467 shorter events, 110.4 us)
Async XLA Ops:
  7.2 48.4 %reduce-scatter.9.cloned.1.call-start = ((), (), s32[]{:S(2)}) async-start(), calls=%async_computation.8 | async-start | bytes 983040 | tf_op jit(solution)/shard_map/reduce_scatter | solution.py:38
  13.7 11.6 %copy-start.29 = (bf16[2,3,768,192]{2,3,1,0:T(8,128)(2,1)S(1)}, bf16[2,3,768,192]{2,3,1,0:T(8,128)(2,1)}, u32[]{:S(2)}) copy-start(bf16[2,3,768,192]{2,3,1,0:T(8,128)(2,1)} %param.27) | copy-start | bytes 5308420
  14.2 12.3 %copy-start.88 = (f32[128]{0:T(128)}, f32[128]{0:T(128)S(1)}, u32[]{:S(2)}) copy-start(f32[128]{0:T(128)S(1)} %broadcast_multiply_fusion.3) | copy-start | bytes 1540
  14.4 12.0 %copy-start.111 = (f32[128]{0:T(128)}, f32[128]{0:T(128)S(1)}, u32[]{:S(2)}) copy-start(f32[128]{0:T(128)S(1)} %fusion.108) | copy-start | bytes 1540
  15.1 83.5 %copy-start.61 = (f32[768]{0:T(1024)}, f32[768]{0:T(1024)S(1)}, u32[]{:S(2)}) copy-start(f32[768]{0:T(1024)S(1)} %get-tuple-element.218) | copy-start | bytes 9220
  31.3 65.9 %reduce-scatter.11.cloned.1.call-start = ((), (), s32[]{:S(2)}) async-start(), calls=%async_computation.9 | async-start | bytes 983040 | tf_op jit(solution)/shard_map/reduce_scatter | solution.py:38
  56.8 14.0 %copy-start.90 = (f32[128]{0:T(128)}, f32[128]{0:T(128)S(1)}, u32[]{:S(2)}) copy-start(f32[128]{0:T(128)S(1)} %broadcast_multiply_fusion.2) | copy-start | bytes 1540
  57.0 13.8 %copy-start.125 = (f32[128]{0:T(128)}, f32[128]{0:T(128)S(1)}, u32[]{:S(2)}) copy-start(f32[128]{0:T(128)S(1)} %multiply_reduce_fusion.4) | copy-start | bytes 1540
  57.0 13.8 %copy-start.113 = (f32[128]{0:T(128)}, f32[128]{0:T(128)S(1)}, u32[]{:S(2)}) copy-start(f32[128]{0:T(128)S(1)} %fusion.109) | copy-start | bytes 1540
  73.4 72.5 %reduce-scatter.13.cloned.1.call-start = ((), (), s32[]{:S(2)}) async-start(), calls=%async_computation.10 | async-start | bytes 983040 | tf_op jit(solution)/shard_map/reduce_scatter | solution.py:38
  122.1 25.8 %copy-start.66 = (f32[768]{0:T(1024)S(1)}, f32[768]{0:T(1024)}, u32[]{:S(2)}) copy-start(f32[768]{0:T(1024)} %get-tuple-element.221) | copy-start | bytes 9220
  122.1 25.8 %copy-start.75 = (f32[768]{0:T(1024)S(1)}, f32[768]{0:T(1024)}, u32[]{:S(2)}) copy-start(f32[768]{0:T(1024)} %get-tuple-element.130) | copy-start | bytes 9220
  122.1 73.8 %reduce-scatter.17.cloned.1.call-start = ((), (), s32[]{:S(2)}) async-start(), calls=%async_computation.12 | async-start | bytes 983040 | tf_op jit(solution)/shard_map/reduce_scatter | solution.py:51
  172.1 49.5 %reduce-scatter.15.cloned.1.call-start = ((), (), s32[]{:S(2)}) async-start(), calls=%async_computation.11 | async-start | bytes 983040 | tf_op jit(solution)/shard_map/reduce_scatter | solution.py:38
  175.4 93.7 %reduce-scatter.19.cloned.1.call-start = ((), (), s32[]{:S(2)}) async-start(), calls=%async_computation.13 | async-start | bytes 983040 | tf_op jit(solution)/shard_map/reduce_scatter | solution.py:51
  221.6 12.2 %copy-start.55 = (bf16[2,192,768]{2,1,0:T(8,128)(2,1)S(1)}, bf16[2,192,768]{2,1,0:T(8,128)(2,1)}, u32[]{:S(2)}) copy-start(bf16[2,192,768]{2,1,0:T(8,128)(2,1)} %param.29) | copy-start | bytes 1769476
  243.5 25.5 %copy-start.62 = (f32[768]{0:T(1024)S(1)}, f32[768]{0:T(1024)}, u32[]{:S(2)}) copy-start(f32[768]{0:T(1024)} %copy-done.61) | copy-start | bytes 9220
  243.5 25.5 %copy-start.93 = (f32[128]{0:T(128)S(1)}, f32[128]{0:T(128)}, u32[]{:S(2)}) copy-start(f32[128]{0:T(128)} %copy-done.92) | copy-start | bytes 1540
  245.2 69.4 %reduce-scatter.21.cloned.1.call-start = ((), (), s32[]{:S(2)}) async-start(), calls=%async_computation.14 | async-start | bytes 983040 | tf_op jit(solution)/shard_map/reduce_scatter | solution.py:51
  269.1 15.6 %copy-start.140 = (f32[512,768]{1,0:T(8,128)S(1)}, f32[512,768]{1,0:T(8,128)}, u32[]{:S(2)}) copy-start(f32[512,768]{1,0:T(8,128)} %get-tuple-element.176) | copy-start | bytes 4718596
  290.8 105.4 %reduce-scatter.23.cloned.1.call-start = ((), (), s32[]{:S(2)}) async-start(), calls=%async_computation.15 | async-start | bytes 983040 | tf_op jit(solution)/shard_map/reduce_scatter | solution.py:51
  290.9 23.7 %copy-start.91 = (f32[128]{0:T(128)S(1)}, f32[128]{0:T(128)}, u32[]{:S(2)}) copy-start(f32[128]{0:T(128)} %copy-done.90) | copy-start | bytes 1540
  290.9 25.5 %copy-start.126 = (f32[128]{0:T(128)S(1)}, f32[128]{0:T(128)}, u32[]{:S(2)}) copy-start(f32[128]{0:T(128)} %copy-done.125) | copy-start | bytes 1540
  290.9 25.5 %copy-start.114 = (f32[128]{0:T(128)S(1)}, f32[128]{0:T(128)}, u32[]{:S(2)}) copy-start(f32[128]{0:T(128)} %copy-done.113) | copy-start | bytes 1540
  337.8 475.6 %all-reduce.9.cloned.1.call-start = ((), (), s32[]{:S(2)}) async-start(), calls=%async_computation.17 | async-start | bytes 28311552 | tf_op jit(solution)/shard_map/psum | solution.py:302
  352.6 43.5 %copy-start.89 = (f32[128]{0:T(128)S(1)}, f32[128]{0:T(128)}, u32[]{:S(2)}) copy-start(f32[128]{0:T(128)} %copy-done.88) | copy-start | bytes 1540
  352.6 45.3 %copy-start.124 = (f32[128]{0:T(128)S(1)}, f32[128]{0:T(128)}, u32[]{:S(2)}) copy-start(f32[128]{0:T(128)} %copy-done.123) | copy-start | bytes 1540
  352.6 45.3 %copy-start.112 = (f32[128]{0:T(128)S(1)}, f32[128]{0:T(128)}, u32[]{:S(2)}) copy-start(f32[128]{0:T(128)} %copy-done.111) | copy-start | bytes 1540
  352.6 47.1 %copy-start.102 = (pred[128]{0:T(512)(128)(4,1)S(1)}, pred[128]{0:T(512)(128)(4,1)}, u32[]{:S(2)}) copy-start(pred[128]{0:T(512)(128)(4,1)} %copy-done.101) | copy-start | bytes 388
  352.6 47.1 %copy-start.105 = (pred[128]{0:T(512)(128)(4,1)S(1)}, pred[128]{0:T(512)(128)(4,1)}, u32[]{:S(2)}) copy-start(pred[128]{0:T(512)(128)(4,1)} %copy-done.104) | copy-start | bytes 388
  352.7 600.9 %all-reduce.7.cloned.1.call-start = ((), (), s32[]{:S(2)}) async-start(), calls=%async_computation.16 | async-start | bytes 4718592 | tf_op jit(solution)/shard_map/psum | solution.py:350
  404.6 44.4 %copy-start.103 = (pred[128]{0:T(512)(128)(4,1)S(1)}, pred[128]{0:T(512)(128)(4,1)}, u32[]{:S(2)}) copy-start(pred[128]{0:T(512)(128)(4,1)} %copy-done.101) | copy-start | bytes 388
  (119 other events, 338.4 us)
Sparse Core Ops, SparseCore 0:
  31.4 24.1 reduce-scatter.8
  73.5 23.6 reduce-scatter.10
  122.2 23.6 reduce-scatter.12
  172.2 23.6 reduce-scatter.16
  198.3 23.2 reduce-scatter.14
  245.4 23.6 reduce-scatter.18
  290.9 23.6 reduce-scatter.20
  337.9 23.6 reduce-scatter.22
  367.7 445.5 all-reduce.8
  819.3 134.2 all-reduce.6
where the time goes:
time: 973 us; the launch traced here: 964 us
  waiting for transfers between devices  637 us (65%)
  blocking collectives  152 us (16%)
  matrix products  68.6 us (7%)
  other arithmetic  54.3 us (6%)
  local copies, waits for them, and re-layouts  36.1 us (4%)
  between operations  16 us (2%)
    psum x1, waiting for transfers between devices, per_device(): lax.psum((grad_attention, grad_attnbias, grad_combiner, grad_expander, gr...  364 us
    psum x1, waiting for transfers between devices, per_device(): lax.psum((grad_scales, grad_shifts, grad_combbias, grad_redbias, grad_pro...  128 us
    reduce_scatter x4, waiting for transfers between devices, sum_forward(): lax.psum_scatter(term(jnp.int32(0), local_rows * lax.axis_size('narrow'))...  82.4 us
    reduce_scatter x4, waiting for transfers between devices, sum_backward(): lax.psum_scatter(term(jnp.int32(0), local_rows * lax.axis_size('narrow'))...  63.6 us
    psum x1, blocking collectives, per_device(): lax.psum((grad_scales, grad_shifts, grad_combbias, grad_redbias, grad_pro...  43.3 us
    psum x1, blocking collectives, per_device(): lax.psum((grad_attention, grad_attnbias, grad_combiner, grad_expander, gr...  38.3 us
    all_gather x4, blocking collectives, share_rows(): return lax.all_gather(values, 'narrow', axis=0, tiled=True)  35.2 us
    all_gather x4, blocking collectives, share_grads(): return lax.all_gather(values, 'narrow', axis=0, tiled=True)  34.9 us
  transfers between devices with their start and end apart: 10, of which 9 were waited for; matrix products, arithmetic and copies ran while one was open for 5% of the time, Pallas kernels for 0%

commit v1 on v0

--- a/solution.py
+++ b/solution.py
@@ -9,6 +9,27 @@
 norm_eps = 1e-06
 
 
+def gather_around(x, axis, dim):
+    size, position, rows = (lax.axis_size(axis), lax.axis_index(axis), x.shape[dim])
+    upward = [(i, (i + 1) % size) for i in range(size)]
+    left = [(i, (i - 1) % size) for i in range(size)]
+    result = jnp.zeros((*x.shape[:dim], size * rows, *x.shape[dim + 1 :]), x.dtype)
+    result = lax.dynamic_update_slice_in_dim(result, x, position * rows, axis=dim)
+    from_left = from_right = x
+    middle = size // 2
+    for turn in range(1, middle + 1):
+        from_left = lax.ppermute(from_left, axis, upward)
+        result = lax.dynamic_update_slice_in_dim(
+            result, from_left, (position - turn) % size * rows, axis=dim
+        )
+        if turn < size - middle:
+            from_right = lax.ppermute(from_right, axis, left)
+            result = lax.dynamic_update_slice_in_dim(
+                result, from_right, (position + turn) % size * rows, axis=dim
+            )
+    return result
+
+
 def normalize(values, gain, shift):
     center = values - jnp.mean(values, axis=-1, keepdims=True)
     variance = jnp.mean(center * center, axis=-1, keepdims=True)
@@ -27,7 +48,7 @@
 
 
 def share_grads(values):
-    return lax.all_gather(values, "narrow", axis=0, tiled=True)
+    return gather_around(values, "narrow", 0)
 
 
 def sum_forward(source, weight, local_rows):

time: 973 us -> 985 us (1.012)
  waiting for transfers between devices: 637 us -> 675 us
  blocking collectives: 152 us -> 116 us
    all_gather x4 -> x0, blocking collectives: 34.9 us -> none  [share_grads(): return lax.all_gather(values, 'narrow', axis=0, tiled=True)]
    ppermute x0 -> x12, waiting for transfers between devices: none -> 31.5 us  [the longest x8 31.5 us: gather_around(): from_left = lax.ppermute(from_left, axis, upward)]
    unnamed x297 -> x279, local copies, waits for them, and re-layouts: 20.8 us -> 18.9 us
  transfers between devices with their start and end apart: 10 -> 22, of which waited for: 9 -> 17; matrix products, arithmetic and copies ran while one was open for 5% -> 5% of each run, Pallas kernels for 0% -> 0%
where the time goes in v1:
time: 985 us; the launch traced here: 976 us
  waiting for transfers between devices  675 us (69%)
  blocking collectives  116 us (12%)
  matrix products  68.2 us (7%)
  other arithmetic  52.5 us (5%)
  local copies, waits for them, and re-layouts  40.7 us (4%)
  between operations  16.1 us (2%)
    psum x1, waiting for transfers between devices, per_device(): lax.psum((grad_attention, grad_attnbias, grad_combiner, grad_expander, gr...  369 us
    psum x1, waiting for transfers between devices, per_device(): lax.psum((grad_scales, grad_shifts, grad_combbias, grad_redbias, grad_pro...  127 us
    reduce_scatter x4, waiting for transfers between devices, sum_forward(): lax.psum_scatter(term(jnp.int32(0), local_rows * lax.axis_size('narrow'))...  80.2 us
    reduce_scatter x4, waiting for transfers between devices, sum_backward(): lax.psum_scatter(term(jnp.int32(0), local_rows * lax.axis_size('narrow'))...  66.7 us
    psum x1, blocking collectives, per_device(): lax.psum((grad_scales, grad_shifts, grad_combbias, grad_redbias, grad_pro...  42.9 us
    psum x1, blocking collectives, per_device(): lax.psum((grad_attention, grad_attnbias, grad_combiner, grad_expander, gr...  38 us
    all_gather x4, blocking collectives, share_rows(): return lax.all_gather(values, 'narrow', axis=0, tiled=True)  35.2 us
    ppermute x8, waiting for transfers between devices, gather_around(): from_left = lax.ppermute(from_left, axis, upward)  31.5 us
  transfers between devices with their start and end apart: 22, of which 17 were waited for; matrix products, arithmetic and copies ran while one was open for 5% of the time, Pallas kernels for 0%

profile of v1, /device:TPU:0, one launch (start us, length us, event | category | flops | bytes accessed | tf_op | source)
XLA Modules:
  0.0 976.2 jit_solution(8696004591237231154)
XLA Ops:
  15.2 10.1 %all_gather.12 = bf16[512,768]{1,0:T(8,128)(2,1)S(1)} all-gather(bf16[128,768]{1,0:T(8,128)(2,1)S(1)} %add_convert_fusion.3), channel_id=1, replica_groups=mesh['wide'=8,'narrow'=4] {'narrow'}, dimensions={0}, use_global_device_ids=true | all-gather | bytes 983040 | tf_op jit(solution)/shard_map/all_gather | solution.py:47
  35.5 23.0 %reduce-scatter.9.cloned.1.call-done = bf16[128,768]{1,0:T(8,128)(2,1)} async-done(((bf16[512,768]{1,0:T(8,128)(2,1)}), bf16[128,768]{1,0:T(8,128)(2,1)}) %reduce-scatter.9.cloned.1.call-update) | async-done | bytes 196624 | tf_op jit(solution)/shard_map/reduce_scatter | solution.py:59
  60.1 8.2 all_gather.13
  68.3 5.4 multiply_convert_fusion.3
  77.1 23.1 %reduce-scatter.11.cloned.1.call-done = bf16[128,768]{1,0:T(8,128)(2,1)} async-done(((bf16[512,768]{1,0:T(8,128)(2,1)}), bf16[128,768]{1,0:T(8,128)(2,1)}) %reduce-scatter.11.cloned.1.call-update) | async-done | bytes 196624 | tf_op jit(solution)/shard_map/reduce_scatter | solution.py:59
  102.2 8.2 all_gather.14
  138.9 11.5 %reduce-scatter.13.cloned.1.call-done = bf16[128,768]{1,0:T(8,128)(2,1)} async-done(((bf16[512,768]{1,0:T(8,128)(2,1)}), bf16[128,768]{1,0:T(8,128)(2,1)}) %reduce-scatter.13.cloned.1.call-update) | async-done | bytes 196624 | tf_op jit(solution)/shard_map/reduce_scatter | solution.py:59
  152.5 8.7 all_gather.15
  161.2 10.9 %multiply_convert_fusion.2 = (bf16[512,768]{1,0:T(8,128)(2,1)}, f32[512,768]{1,0:T(8,128)S(1)}, f32[512,768]{1,0:T(8,128)S(1)}) fusion(f32[768]{0:T(1024)S(1)} %copy-done.108, bf16[512,768]{1,0:T(8,128)(2,1)S(1)} %all_gather.15, bf16[2,768,768]{2,1,0:T(8,128)(2,1)S(1)} %copy-done.122), kind=kOutput, calls=%fused_computation.19 | convolution fusion | flops 629932032 | bytes 5902336 | tf_op jit(solution)/shard_map/dot_general | solution.py:200
  172.2 2.9 fusion.134
  177.8 3.2 convolution_convert_fusion.2
  181.0 20.5 %reduce-scatter.17.cloned.1.call-done = bf16[128,768]{1,0:T(8,128)(2,1)} async-done(((bf16[512,768]{1,0:T(8,128)(2,1)}), bf16[128,768]{1,0:T(8,128)(2,1)}) %reduce-scatter.17.cloned.1.call-update) | async-done | bytes 196624 | tf_op jit(solution)/shard_map/reduce_scatter | solution.py:72
  204.6 22.6 %reduce-scatter.15.cloned.1.call-done = bf16[128,768]{1,0:T(8,128)(2,1)} async-done(((bf16[512,768]{1,0:T(8,128)(2,1)}), bf16[128,768]{1,0:T(8,128)(2,1)}) %reduce-scatter.15.cloned.1.call-update) | async-done | bytes 196624 | tf_op jit(solution)/shard_map/reduce_scatter | solution.py:59
  232.0 4.9 collective-permute-done.3
  237.0 5.0 collective-permute-done.5
  245.6 2.7 convert_reduce_fusion.5
  254.4 23.1 %reduce-scatter.19.cloned.1.call-done = bf16[128,768]{1,0:T(8,128)(2,1)} async-done(((bf16[512,768]{1,0:T(8,128)(2,1)}), bf16[128,768]{1,0:T(8,128)(2,1)}) %reduce-scatter.19.cloned.1.call-update) | async-done | bytes 196624 | tf_op jit(solution)/shard_map/reduce_scatter | solution.py:72
  286.5 4.9 collective-permute-done.6
  291.6 5.0 collective-permute-done.8
  301.2 23.0 %reduce-scatter.21.cloned.1.call-done = bf16[128,768]{1,0:T(8,128)(2,1)} async-done(((bf16[512,768]{1,0:T(8,128)(2,1)}), bf16[128,768]{1,0:T(8,128)(2,1)}) %reduce-scatter.21.cloned.1.call-update) | async-done | bytes 196624 | tf_op jit(solution)/shard_map/reduce_scatter | solution.py:72
  333.8 2.7 collective-permute-done.9
  336.6 5.0 collective-permute-done.11
  350.3 3.7 convolution_bitcast_fusion
  366.5 38.0 %all-reduce.2 = (f32[1,2,192]{2,1,0:T(2,128)S(1)}, f32[1,2,192]{2,1,0:T(2,128)S(1)}, f32[1,768]{1,0:T(1,128)S(1)}, f32[1,768]{1,0:T(1,128)S(1)}) all-reduce(f32[1,2,192]{2,1,0:T(2,128)S(1)} %maximum_bitcast_fusion.5, f32[1,2,192]{2,1,0:T(2,128)S(1)} %maximum_bitcast_fusion.4, ...), channel_id=1, replica_groups=mesh['wide'=8,'narrow'=4] {'wide'}, use_global_device_ids=true, to_apply=%region_56.57 | all-reduce | flops 2304 | bytes 18432 | tf_op jit(solution)/shard_map/psum | solution.py:323
  412.3 42.9 %all-reduce = (f32[2,768]{1,0:T(2,128)}, f32[768]{0:T(1024)}, f32[2,2,768]{2,1,0:T(2,128)}, f32[2,2,768]{2,1,0:T(2,128)}, f32[2,768]{1,0:T(2,128)}, /*index=5*/f32[2,768]{1,0:T(2,128)}) all-reduce(f32[2,768]{1,0:T(2,128)S(1)} %pad_maximum_fusion.9, ...), channel_id=1, replica_groups=mesh['wide'=8,'narrow'=4] {'wide','narrow'}, use_global_device_ids=true, to_apply=%region_34.35 | all-reduce | flops 11520 | bytes 92160 | tf_op jit(solution)/shard_map/psum | solution.py:371
  456.3 368.9 %all-reduce.9.cloned.1.call-done = (f32[1,3,768,192]{2,3,1,0:T(8,128)}, f32[1,3,768,192]{2,3,1,0:T(8,128)}, f32[1,192,768]{2,1,0:T(8,128)}, f32[1,192,768]{2,1,0...) async-done(((f32[1,3,768,192]{2,3,1,0:T(8,128)}, f32[1,3,768,192]{2,3,1,0:T(8,128)}, ...) | async-done | bytes 14155792 | tf_op jit(solution)/shard_map/psum | solution.py:323
  825.2 2.5 pad_maximum_fusion.3
  827.7 3.8 pad_maximum_fusion.2
  831.5 2.7 pad_maximum_fusion
  835.6 2.5 pad_maximum_fusion.1
  838.1 127.4 %all-reduce.7.cloned.1.call-done = (f32[2,256,768]{2,1,0:T(8,128)}, f32[256,768]{1,0:T(8,128)}) async-done(((f32[2,256,768]{2,1,0:T(8,128)}, f32[256,768]{1,0:T(8,128)}), (f32[2,256,768]{2,1,0:T(8,128)}, f32[256,768]{1,0:T(8,128)})) %all-reduce.7.cloned.1.call-update) | async-done | bytes 2359312 | tf_op jit(solution)/shard_map/psum | solution.py:371
  965.5 2.7 copy.226
  (486 shorter events, 130.4 us)
Async XLA Ops:
  7.2 51.3 %reduce-scatter.9.cloned.1.call-start = ((), (), s32[]{:S(2)}) async-start(), calls=%async_computation.8 | async-start | bytes 983040 | tf_op jit(solution)/shard_map/reduce_scatter | solution.py:59
  15.1 87.0 %copy-start.59 = (f32[768]{0:T(1024)}, f32[768]{0:T(1024)S(1)}, u32[]{:S(2)}) copy-start(f32[768]{0:T(1024)S(1)} %get-tuple-element.224) | copy-start | bytes 9220
  34.3 65.9 %reduce-scatter.11.cloned.1.call-start = ((), (), s32[]{:S(2)}) async-start(), calls=%async_computation.9 | async-start | bytes 983040 | tf_op jit(solution)/shard_map/reduce_scatter | solution.py:59
  76.4 74.0 %reduce-scatter.13.cloned.1.call-start = ((), (), s32[]{:S(2)}) async-start(), calls=%async_computation.10 | async-start | bytes 983040 | tf_op jit(solution)/shard_map/reduce_scatter | solution.py:59
  126.5 75.0 %reduce-scatter.17.cloned.1.call-start = ((), (), s32[]{:S(2)}) async-start(), calls=%async_computation.12 | async-start | bytes 983040 | tf_op jit(solution)/shard_map/reduce_scatter | solution.py:72
  126.6 6.3 collective-permute-start
  127.0 7.5 collective-permute-start.1
  132.9 5.3 collective-permute-start.2
  177.7 49.5 %reduce-scatter.15.cloned.1.call-start = ((), (), s32[]{:S(2)}) async-start(), calls=%async_computation.11 | async-start | bytes 983040 | tf_op jit(solution)/shard_map/reduce_scatter | solution.py:59
  177.8 49.4 %copy-start.73 = (f32[768]{0:T(1024)S(1)}, f32[768]{0:T(1024)}, u32[]{:S(2)}) copy-start(f32[768]{0:T(1024)} %get-tuple-element.134) | copy-start | bytes 9220
  181.0 96.5 %reduce-scatter.19.cloned.1.call-start = ((), (), s32[]{:S(2)}) async-start(), calls=%async_computation.13 | async-start | bytes 983040 | tf_op jit(solution)/shard_map/reduce_scatter | solution.py:72
  230.2 6.7 collective-permute-start.3
  230.3 6.6 collective-permute-start.4
  236.9 5.1 collective-permute-start.5
  252.6 24.9 %copy-start.89 = (f32[128]{0:T(128)S(1)}, f32[128]{0:T(128)}, u32[]{:S(2)}) copy-start(f32[128]{0:T(128)} %copy-done.88) | copy-start | bytes 1540
  254.3 69.9 %reduce-scatter.21.cloned.1.call-start = ((), (), s32[]{:S(2)}) async-start(), calls=%async_computation.14 | async-start | bytes 983040 | tf_op jit(solution)/shard_map/reduce_scatter | solution.py:72
  284.7 6.7 collective-permute-start.6
  284.7 6.8 collective-permute-start.7
  291.4 5.2 collective-permute-start.8
  299.3 26.6 %copy-start.115 = (f32[128]{0:T(128)S(1)}, f32[128]{0:T(128)}, u32[]{:S(2)}) copy-start(f32[128]{0:T(128)} %copy-done.114) | copy-start | bytes 1540
  299.3 26.6 %copy-start.103 = (f32[128]{0:T(128)S(1)}, f32[128]{0:T(128)}, u32[]{:S(2)}) copy-start(f32[128]{0:T(128)} %copy-done.102) | copy-start | bytes 1540
  301.1 104.6 %reduce-scatter.23.cloned.1.call-start = ((), (), s32[]{:S(2)}) async-start(), calls=%async_computation.15 | async-start | bytes 983040 | tf_op jit(solution)/shard_map/reduce_scatter | solution.py:72
  329.8 6.7 collective-permute-start.9
  329.9 6.6 collective-permute-start.10
  336.5 5.1 collective-permute-start.11
  350.3 474.9 %all-reduce.9.cloned.1.call-start = ((), (), s32[]{:S(2)}) async-start(), calls=%async_computation.17 | async-start | bytes 28311552 | tf_op jit(solution)/shard_map/psum | solution.py:323
  365.3 40.4 %copy-start.85 = (f32[128]{0:T(128)S(1)}, f32[128]{0:T(128)}, u32[]{:S(2)}) copy-start(f32[128]{0:T(128)} %copy-done.84) | copy-start | bytes 1540
  365.3 41.5 %copy-start.113 = (f32[128]{0:T(128)S(1)}, f32[128]{0:T(128)}, u32[]{:S(2)}) copy-start(f32[128]{0:T(128)} %copy-done.112) | copy-start | bytes 1540
  365.3 41.5 %copy-start.101 = (f32[128]{0:T(128)S(1)}, f32[128]{0:T(128)}, u32[]{:S(2)}) copy-start(f32[128]{0:T(128)} %copy-done.100) | copy-start | bytes 1540
  365.3 42.8 %copy-start.94 = (pred[128]{0:T(512)(128)(4,1)S(1)}, pred[128]{0:T(512)(128)(4,1)}, u32[]{:S(2)}) copy-start(pred[128]{0:T(512)(128)(4,1)} %copy-done.93) | copy-start | bytes 388
  365.3 42.8 %copy-start.96 = (pred[128]{0:T(512)(128)(4,1)S(1)}, pred[128]{0:T(512)(128)(4,1)}, u32[]{:S(2)}) copy-start(pred[128]{0:T(512)(128)(4,1)} %copy-done.95) | copy-start | bytes 388
  365.4 600.1 %all-reduce.7.cloned.1.call-start = ((), (), s32[]{:S(2)}) async-start(), calls=%async_computation.16 | async-start | bytes 4718592 | tf_op jit(solution)/shard_map/psum | solution.py:371
  (122 other events, 533.2 us)
Sparse Core Ops, SparseCore 0:
  34.4 24.1 reduce-scatter.8
  76.5 23.6 reduce-scatter.10
  126.6 23.6 reduce-scatter.12
  177.9 23.6 reduce-scatter.16
  203.9 23.2 reduce-scatter.14
  254.5 23.0 reduce-scatter.18
  301.2 22.9 reduce-scatter.20
  350.4 23.0 reduce-scatter.22
  379.6 445.5 all-reduce.8
  831.2 134.2 all-reduce.6
